TPU v7x, 32 devices: a whole 2x2x4 slice. The times are simulated.
32 devices in a mesh: dev: 32 (over z, y, x, core).
Axes of the slice: x: 2, y: 2, z: 4, core: 2. Of those that a mesh axis runs over, the one named last changes fastest.
Arguments:
- tensor_tiles: bfloat16 [128, 64, 128, 128], P('dev'), may hold values from -196608 to 196608
- tile_coords: int32 [128, 3], P('dev'), may hold values from 0 to 31, as said below
- tile_count: int32 [32], P('dev'), may hold values from 1 to 4, as said below
- owned_i: int32 [32], P('dev'), may hold values from 0 to 31, as said below
- owned_j: int32 [32], P('dev'), may hold values from 0 to 31, as said below
- owned_k: int32 [32], P('dev'), may hold values from 0 to 31, as said below
- factor_a: float32 [32, 64, 512], P('dev'), may hold values from 0 to 7
- factor_b: float32 [32, 128, 512], P('dev'), may hold values from 0 to 7
- factor_c: float32 [32, 128, 512], P('dev'), may hold values from 0 to 7
- dual_a: float32 [32, 64, 512], P('dev'), may hold values from -1.75 to 1.75
- dual_b: float32 [32, 128, 512], P('dev'), may hold values from -1.75 to 1.75
- dual_c: float32 [32, 128, 512], P('dev'), may hold values from -1.75 to 1.75
- penalty: float32 [3], replicated, may hold values from 0.5 to 2
Outputs:
- factor_a_new: float32 [32, 64, 512], P('dev')
- dual_a_new: float32 [32, 64, 512], P('dev')
- factor_b_new: float32 [32, 128, 512], P('dev')
- dual_b_new: float32 [32, 128, 512], P('dev')
- factor_c_new: float32 [32, 128, 512], P('dev')
- dual_c_new: float32 [32, 128, 512], P('dev')
Inputs may be any that keep to these rules, and one draw needn't show every extreme that they name: `owned_i`: each block number appears once. `owned_j`: each block number appears once. `owned_k`: each block number appears once. `tile_coords`: for a live slot on device d, the block named for each mode is owned by a device d + o with o between -2 and 2, counted around the axis; slots may name the same blocks, and their tiles then add; slots that are not live hold arbitrary block numbers. `tile_count`: some device has all 4 slots live.
All inputs are finite; a program needn't handle non-finite values.
Results may differ from a plain program's by a relative error of at most 0.0025.
The roundings to bfloat16 on the way count: a program that leaves them out, or rounds other values in their place, can miss the bound.
Values may be sent and summed in bfloat16 or wider, within the bound.
A program may use at most 128 MiB of HBM per device.

v0:
```python
import jax
import jax.numpy as jnp
from jax import lax
from jax.sharding import PartitionSpec as P

ITERS = 6
REACH = 2


def for_sending(array):
    return jax.tree.map(lambda a: a.astype(jnp.bfloat16) if a.dtype == jnp.float32 else a, array)


def passed_along(block, axis, distance):
    devices = range(lax.axis_size(axis))
    route = [((i - distance) % len(devices), i) for i in devices]
    return lax.ppermute(block, axis, route)


def chol_solve(chol_low, right_side):
    middle = lax.linalg.triangular_solve(chol_low, right_side, left_side=True, lower=True)
    return lax.linalg.triangular_solve(
        chol_low, middle, left_side=True, lower=True, transpose_a=True
    )


def gram_local(factor):
    flat_rows = factor.reshape(-1, factor.shape[-1])
    return lax.dot_general(
        flat_rows,
        flat_rows,
        (((0,), (0,)), ((), ())),
        precision=lax.Precision.HIGHEST,
        preferred_element_type=jnp.float32,
    )


def window_offsets():
    offsets = [0]
    for distance in range(1, REACH + 1):
        offsets.append(distance)
        offsets.append(-distance)
    return offsets


def neighbour(payload, offset):
    return jax.tree.map(
        lambda part, own: part.astype(own.dtype),
        passed_along(for_sending(payload), "dev", -offset),
        payload,
    )


def expand(payload):
    result = [payload]
    for offset in window_offsets()[1:]:
        result.append(neighbour(payload, offset))
    return result


def fold(totals):
    offsets = window_offsets()
    result = totals[0]
    for place_index in range(1, len(offsets)):
        result = result + passed_along(totals[place_index], "dev", offsets[place_index])
    return result


def position(window_ids, block_id):
    return jnp.sum(
        jnp.where(window_ids == block_id, jnp.arange(window_ids.shape[0], dtype=jnp.int32), 0)
    )


def admm_update(mttkrp, factor, dual_var, gram_mat, weight):
    rank_size = gram_mat.shape[0]
    rho_value = weight * jnp.trace(gram_mat) / rank_size
    identity = jnp.eye(rank_size, dtype=jnp.float32)
    chol_low = jnp.linalg.cholesky(gram_mat + rho_value * identity)
    inverse = chol_solve(chol_low, identity)
    for sweep_index in range(ITERS):
        auxiliary = jnp.dot(
            mttkrp + rho_value * (factor + dual_var),
            inverse,
            precision=lax.Precision.HIGHEST,
            preferred_element_type=jnp.float32,
        )
        factor = jnp.maximum(auxiliary - dual_var, 0.0)
        dual_var = dual_var + factor - auxiliary
    return (factor, dual_var)


def per_device(
    tensor_tiles,
    tile_coords,
    tile_count,
    owned_i,
    owned_j,
    owned_k,
    factor_a,
    factor_b,
    factor_c,
    dual_a,
    dual_b,
    dual_c,
    penalty,
):
    slot_count, rows_first, rows_second, rows_third = tensor_tiles.shape
    rank_size = factor_a.shape[2]
    count_live = tile_count[0]
    win_count = len(window_offsets())
    gram_b, gram_c = lax.psum((gram_local(factor_b), gram_local(factor_c)), "dev")
    own_ids = jnp.concatenate([owned_i, owned_j, owned_k])
    first_window = expand(
        (factor_b[0].astype(jnp.bfloat16), factor_c[0].astype(jnp.bfloat16), own_ids)
    )
    win_b = jnp.stack([member[0] for member in first_window])
    win_c = jnp.stack([member[1] for member in first_window])
    ids_window = jnp.stack([member[2] for member in first_window])

    def slice_tile(slot_index):
        return lax.dynamic_index_in_dim(tensor_tiles, slot_index, 0, keepdims=False)

    def first_part(tile_now, coord_row):
        third_rows = win_c[position(ids_window[:, 2], coord_row[2])]
        flat_tile = tile_now.reshape(rows_first * rows_second, rows_third)
        partial_value = jnp.dot(flat_tile, third_rows, preferred_element_type=jnp.float32)
        return partial_value.reshape(rows_first, rows_second, rank_size)

    def mode_first(slot_index, loop_carry):
        totals = loop_carry[0]
        coord_row = tile_coords[slot_index]
        partial_value = first_part(slice_tile(slot_index), coord_row)
        second_rows = win_b[position(ids_window[:, 1], coord_row[1])]
        contrib = jnp.sum(partial_value * second_rows[None, :, :], axis=1)
        totals = totals.at[position(ids_window[:, 0], coord_row[0])].add(contrib)
        return (totals,)

    start_first = jnp.zeros((win_count, rows_first, rank_size), jnp.float32)
    first_carry = (start_first,)
    first_result = lax.fori_loop(0, count_live, mode_first, first_carry)
    mttkrp_a = fold(first_result[0])
    factor_a_new, dual_a_new = admm_update(
        mttkrp_a, factor_a[0], dual_a[0], gram_b * gram_c, penalty[0]
    )
    gram_a = lax.psum(gram_local(factor_a_new), "dev")
    second_window = expand((factor_a_new.astype(jnp.bfloat16),))
    win_a = jnp.stack([member[0] for member in second_window])

    def mode_second(slot_index, loop_carry):
        totals = loop_carry[0]
        coord_row = tile_coords[slot_index]
        partial_value = first_part(slice_tile(slot_index), coord_row)
        first_rows = win_a[position(ids_window[:, 0], coord_row[0])]
        contrib = jnp.sum(partial_value * first_rows[:, None, :], axis=0)
        totals = totals.at[position(ids_window[:, 1], coord_row[1])].add(contrib)
        return (totals,) + tuple(loop_carry[1:])

    second_carry = (jnp.zeros((win_count, rows_second, rank_size), jnp.float32),) + tuple(
        first_result[1:]
    )
    second_result = lax.fori_loop(0, count_live, mode_second, second_carry)
    mttkrp_b = fold(second_result[0])
    factor_b_new, dual_b_new = admm_update(
        mttkrp_b, factor_b[0], dual_b[0], gram_a * gram_c, penalty[1]
    )
    gram_bn = lax.psum(gram_local(factor_b_new), "dev")
    third_window = expand((factor_b_new.astype(jnp.bfloat16),))
    win_bn = jnp.stack([member[0] for member in third_window])

    def mode_third(slot_index, loop_carry):
        totals = loop_carry[0]
        coord_row = tile_coords[slot_index]
        tile_now = slice_tile(slot_index)
        first_rows = win_a[position(ids_window[:, 0], coord_row[0])]
        flat_tile = tile_now.reshape(rows_first, rows_second * rows_third)
        crossed = lax.dot_general(
            flat_tile, first_rows, (((0,), (0,)), ((), ())), preferred_element_type=jnp.float32
        )
        crossed = crossed.reshape(rows_second, rows_third, rank_size)
        second_rows = win_bn[position(ids_window[:, 1], coord_row[1])]
        contrib = jnp.sum(crossed * second_rows[:, None, :], axis=0)
        totals = totals.at[position(ids_window[:, 2], coord_row[2])].add(contrib)
        return (totals,)

    third_result = lax.fori_loop(
        0, count_live, mode_third, (jnp.zeros((win_count, rows_third, rank_size), jnp.float32),)
    )
    mttkrp_c = fold(third_result[0])
    factor_c_new, dual_c_new = admm_update(
        mttkrp_c, factor_c[0], dual_c[0], gram_a * gram_bn, penalty[2]
    )
    return (
        factor_a_new[None],
        dual_a_new[None],
        factor_b_new[None],
        dual_b_new[None],
        factor_c_new[None],
        dual_c_new[None],
    )


def solution(mesh):
    return jax.shard_map(
        per_device,
        mesh=mesh,
        in_specs=(
            P("dev", None, None, None),
            P("dev", None),
            P("dev"),
            P("dev"),
            P("dev"),
            P("dev"),
            P("dev", None, None),
            P("dev", None, None),
            P("dev", None, None),
            P("dev", None, None),
            P("dev", None, None),
            P("dev", None, None),
            P(),
        ),
        out_specs=(
            P("dev", None, None),
            P("dev", None, None),
            P("dev", None, None),
            P("dev", None, None),
            P("dev", None, None),
            P("dev", None, None),
        ),
        check_vma=False,
    )
```

profile of v0, /device:TPU:0, one launch (start us, length us, event | category | flops | bytes accessed | tf_op | source)
XLA Modules:
  0.0 1002.3 jit_solution(10114383606782808656)
XLA Ops:
  9.2 6.4 collective-permute-start
  18.6 8.4 collective-permute-start.4
  36.3 8.3 collective-permute-start.8
  47.7 7.3 collective-permute-done.9
  56.0 30.8 %while.45 = (s32[]{:T(128)}, f32[5,64,512]{2,1,0:T(8,128)S(1)}, s32[]{:T(128)}, s32[5,3]{0,1:T(4,128)S(1)}, s32[4,3]{1,0:T(4,128)S(1)}, /*index=5*/bf16[4,64,128...) while((s32[]{:T(128)}, f32[5,64,512]{2,1,0:T(8,128)S(1)}, ...), condition=%wide.region_6.7_spmd, body=%wide.region_0.6_spmd.sunk | while | flops 1082228736 | bytes 3408315 | solution.py:141
  87.7 33.0 %collective-permute-start.12 = (f32[64,512]{1,0:T(8,128)S(1)}, f32[64,512]{1,0:T(8,128)S(1)}, u32[]{:S(2)}, u32[]{:S(2)}) collective-permute-start(f32[64,512]{1,0:T(8,128)S(1)} %get-tuple-element.389), channel_id=1, source_target_pairs={{31,0},{0,1},{1,2},{2,3},{3,4},{4,5},{5,6},{6,7},{7,8},{8,9},{9,10... | collective-permute-start | bytes 393224 | tf_op jit(solution)/shard_map/ppermute | solution.py:17
  122.4 4.4 collective-permute-start.15
  131.0 36.6 %all-reduce.10.cloned.1.call-done = (f32[512,512]{0,1:T(8,128)}, f32[512,512]{0,1:T(8,128)}) async-done(((f32[512,512]{0,1:T(8,128)}, f32[512,512]{0,1:T(8,128)}), (f32[512,512]{0,1:T(8,128)}, f32[512,512]{0,1:T(8,128)})) %all-reduce.10.cloned.1.call-update) | async-done | bytes 2097168 | tf_op jit(solution)/shard_map/psum | solution.py:112
  175.1 11.7 %cholesky.374 = f32[128,128]{1,0:T(8,128)S(1)} custom-call(f32[128,128]{1,0:T(8,128)S(1)} %cholesky.586), custom_call_target="Cholesky" | custom-call | tf_op jit(solution)/shard_map/jit(cholesky)/cholesky | solution.py:79
  186.9 9.8 custom-call.36
  199.3 11.7 %cholesky.393 = f32[128,128]{1,0:T(8,128)S(1)} custom-call(f32[128,128]{1,0:T(8,128)S(1)} %cholesky.590), custom_call_target="Cholesky" | custom-call | tf_op jit(solution)/shard_map/jit(cholesky)/cholesky | solution.py:79
  211.1 10.0 custom-call.37
  222.6 11.7 %cholesky.414 = f32[128,128]{1,0:T(8,128)S(1)} custom-call(f32[128,128]{1,0:T(8,128)S(1)} %cholesky.595), custom_call_target="Cholesky" | custom-call | tf_op jit(solution)/shard_map/jit(cholesky)/cholesky | solution.py:79
  235.0 9.8 custom-call.38
  246.3 11.7 %cholesky.431 = f32[128,128]{1,0:T(8,128)S(1)} custom-call(f32[128,128]{1,0:T(8,128)S(1)} %convolution_subtract_fusion.26), custom_call_target="Cholesky" | custom-call | tf_op jit(solution)/shard_map/jit(cholesky)/cholesky | solution.py:79
  262.1 8.0 while.48
  270.1 39.7 %custom-call.40 = f32[4,128,128]{1,2,0:T(8,128)S(1)} custom-call(f32[4,128,128]{2,1,0:T(8,128)S(1)} %get-tuple-element.218), custom_call_target="InvertDiagBlocksLowerTriangular" | custom-call | tf_op jit(solution)/shard_map/triangular_solve/custom-call.8 | solution.py:22
  327.7 5.2 collective-permute-done.17
  335.7 30.8 %while.46 = (s32[]{:T(128)}, f32[5,128,512]{2,1,0:T(8,128)S(1)}, s32[]{:T(128)}, s32[5,3]{0,1:T(4,128)S(1)}, s32[4,3]{1,0:T(4,128)S(1)}, /*index=5*/bf16[4,64,12...) while((s32[]{:T(128)}, f32[5,128,512]{2,1,0:T(8,128)S(1)}, ...), condition=%wide.region_24.28_spmd, body=%wide.region_18.27_spmd.sunk | while | flops 1082228736 | bytes 3604923 | solution.py:162
  358.4 3.9 multiply_reduce_fusion.7
  368.2 32.2 %collective-permute-start.20 = (f32[128,512]{1,0:T(8,128)}, f32[128,512]{1,0:T(8,128)}, u32[]{:S(2)}, u32[]{:S(2)}) collective-permute-start(f32[128,512]{1,0:T(8,128)} %get-tuple-element.383), channel_id=1, source_target_pairs={{31,0},{0,1},{1,2},{2,3},{3,4},{4,5},{5,6},{6,7},{7,8},{8,9},{9,10... | collective-permute-start | bytes 786440 | tf_op jit(solution)/shard_map/ppermute | solution.py:17
  402.0 4.0 collective-permute-start.23
  408.1 5.0 collective-permute-done.22
  418.1 118.1 %all-reduce.6.cloned.1.call-done = f32[512,512]{0,1:T(8,128)} async-done(((f32[512,512]{0,1:T(8,128)}), f32[512,512]{0,1:T(8,128)}) %all-reduce.6.cloned.1.call-update) | async-done | bytes 1048592 | tf_op jit(solution)/shard_map/psum | solution.py:146
  543.4 11.7 %cholesky.446 = f32[128,128]{1,0:T(8,128)S(1)} custom-call(f32[128,128]{1,0:T(8,128)S(1)} %cholesky.599), custom_call_target="Cholesky" | custom-call | tf_op jit(solution)/shard_map/jit(cholesky)/cholesky | solution.py:79
  555.3 9.8 custom-call.41
  567.6 11.7 %cholesky.465 = f32[128,128]{1,0:T(8,128)S(1)} custom-call(f32[128,128]{1,0:T(8,128)S(1)} %cholesky.603), custom_call_target="Cholesky" | custom-call | tf_op jit(solution)/shard_map/jit(cholesky)/cholesky | solution.py:79
  580.7 10.2 %custom-call.42 = f32[1,128,128]{1,2,0:T(8,128)S(1)} custom-call(f32[1,128,128]{2,1,0:T(8,128)S(1)} %get-tuple-element.413), custom_call_target="InvertDiagBlocksLowerTriangular" | custom-call | tf_op jit(solution)/shard_map/jit(cholesky)/cholesky | solution.py:79
  592.4 11.7 %cholesky.486 = f32[128,128]{1,0:T(8,128)S(1)} custom-call(f32[128,128]{1,0:T(8,128)S(1)} %cholesky.608), custom_call_target="Cholesky" | custom-call | tf_op jit(solution)/shard_map/jit(cholesky)/cholesky | solution.py:79
  604.8 9.8 custom-call.43
  616.1 11.9 %cholesky.503 = f32[128,128]{1,0:T(8,128)S(1)} custom-call(f32[128,128]{1,0:T(8,128)S(1)} %convolution_subtract_fusion.25), custom_call_target="Cholesky" | custom-call | tf_op jit(solution)/shard_map/jit(cholesky)/cholesky | solution.py:79
  631.5 8.0 while.49
  639.5 39.3 %custom-call.45 = f32[4,128,128]{1,2,0:T(8,128)S(1)} custom-call(f32[4,128,128]{2,1,0:T(8,128)S(1)} %get-tuple-element.220), custom_call_target="InvertDiagBlocksLowerTriangular" | custom-call | tf_op jit(solution)/shard_map/triangular_solve/custom-call.8 | solution.py:22
  704.3 40.4 %while.47 = (s32[]{:T(128)}, f32[5,128,512]{2,1,0:T(8,128)S(1)}, s32[]{:T(128)}, s32[5,3]{0,1:T(4,128)S(1)}, s32[4,3]{1,0:T(4,128)S(1)}, /*index=5*/bf16[4,64,12...) while((s32[]{:T(128)}, f32[5,128,512]{2,1,0:T(8,128)S(1)}, ...), condition=%wide.region_33.37_spmd, body=%wide.region_27.36_spmd.sunk | while | flops 1090650112 | bytes 8061371 | solution.py:186
  714.3 6.8 multiply_reduce_fusion.8
  734.2 6.8 multiply_reduce_fusion.8
  744.8 42.1 %collective-permute-start.28 = (f32[128,512]{1,0:T(8,128)S(1)}, f32[128,512]{1,0:T(8,128)S(1)}, u32[]{:S(2)}, u32[]{:S(2)}) collective-permute-start(f32[128,512]{1,0:T(8,128)S(1)} %get-tuple-element.379), channel_id=1, source_target_pairs={{31,0},{0,1},{1,2},{2,3},{3,4},{4,5},{5,6},{6,7},{7,8},{8,9},{9,10... | collective-permute-start | bytes 786440 | tf_op jit(solution)/shard_map/ppermute | solution.py:17
  794.1 5.3 collective-permute-done.30
  802.8 36.4 %all-reduce.8.cloned.1.call-done = f32[512,512]{0,1:T(8,128)} async-done(((f32[512,512]{0,1:T(8,128)}), f32[512,512]{0,1:T(8,128)}) %all-reduce.8.cloned.1.call-update) | async-done | bytes 1048592 | tf_op jit(solution)/shard_map/psum | solution.py:167
  846.4 11.7 %cholesky.518 = f32[128,128]{1,0:T(8,128)S(1)} custom-call(f32[128,128]{1,0:T(8,128)S(1)} %cholesky.612), custom_call_target="Cholesky" | custom-call | tf_op jit(solution)/shard_map/jit(cholesky)/cholesky | solution.py:79
  858.3 9.8 custom-call.46
  870.6 11.7 %cholesky.537 = f32[128,128]{1,0:T(8,128)S(1)} custom-call(f32[128,128]{1,0:T(8,128)S(1)} %cholesky.616), custom_call_target="Cholesky" | custom-call | tf_op jit(solution)/shard_map/jit(cholesky)/cholesky | solution.py:79
  883.7 10.0 custom-call.47
  895.2 11.7 %cholesky.558 = f32[128,128]{1,0:T(8,128)S(1)} custom-call(f32[128,128]{1,0:T(8,128)S(1)} %cholesky.621), custom_call_target="Cholesky" | custom-call | tf_op jit(solution)/shard_map/jit(cholesky)/cholesky | solution.py:79
  907.6 9.8 custom-call.48
  918.9 11.9 %cholesky.575 = f32[128,128]{1,0:T(8,128)S(1)} custom-call(f32[128,128]{1,0:T(8,128)S(1)} %convolution_subtract_fusion.24), custom_call_target="Cholesky" | custom-call | tf_op jit(solution)/shard_map/jit(cholesky)/cholesky | solution.py:79
  934.3 8.5 while.50
  942.8 39.3 %custom-call.50 = f32[4,128,128]{1,2,0:T(8,128)S(1)} custom-call(f32[4,128,128]{2,1,0:T(8,128)S(1)} %get-tuple-element.222), custom_call_target="InvertDiagBlocksLowerTriangular" | custom-call | tf_op jit(solution)/shard_map/triangular_solve/custom-call.8 | solution.py:22
  (369 shorter events, 214.0 us)
Async XLA Ops:
  7.2 160.4 %all-reduce.10.cloned.1.call-start = ((), (), s32[]{:S(2)}) async-start(), calls=%async_computation.2 | async-start | bytes 4194304 | tf_op jit(solution)/shard_map/psum | solution.py:112
  9.2 25.0 %collective-permute-start = (s32[3]{0:T(128)S(1)}, s32[3]{0:T(128)S(1)}, u32[]{:S(2)}, u32[]{:S(2)}) collective-permute-start(s32[3]{0:T(128)S(1)} %pad_add_fusion), channel_id=1, source_target_pairs={{1,0},{2,1},{3,2},{4,3},{5,4},{6,5},{7,6},{8,7},{9,8},{10,9},{11,1... | collective-permute-start | bytes 44 | tf_op jit(solution)/shard_map/ppermute | solution.py:17
  15.6 18.6 %collective-permute-start.1 = (s32[3]{0:T(128)S(1)}, s32[3]{0:T(128)S(1)}, u32[]{:S(2)}, u32[]{:S(2)}) collective-permute-start(s32[3]{0:T(128)S(1)} %pad_add_fusion), channel_id=1, source_target_pairs={{31,0},{0,1},{1,2},{2,3},{3,4},{4,5},{5,6},{6,7},{7,8},{8,9},{9,10... | collective-permute-start | bytes 44 | tf_op jit(solution)/shard_map/ppermute | solution.py:17
  15.6 19.0 %collective-permute-start.2 = (s32[3]{0:T(128)S(1)}, s32[3]{0:T(128)S(1)}, u32[]{:S(2)}, u32[]{:S(2)}) collective-permute-start(s32[3]{0:T(128)S(1)} %pad_add_fusion), channel_id=1, source_target_pairs={{2,0},{3,1},{4,2},{5,3},{6,4},{7,5},{8,6},{9,7},{10,8},{11,9},{12,... | collective-permute-start | bytes 44 | tf_op jit(solution)/shard_map/ppermute | solution.py:17
  16.7 19.6 %collective-permute-start.3 = (s32[3]{0:T(128)S(1)}, s32[3]{0:T(128)S(1)}, u32[]{:S(2)}, u32[]{:S(2)}) collective-permute-start(s32[3]{0:T(128)S(1)} %pad_add_fusion), channel_id=1, source_target_pairs={{30,0},{31,1},{0,2},{1,3},{2,4},{3,5},{4,6},{5,7},{6,8},{7,9},{8,1... | collective-permute-start | bytes 44 | tf_op jit(solution)/shard_map/ppermute | solution.py:17
  18.6 14.7 %copy-start.7 = (f32[1,128,512]{2,1,0:T(8,128)S(1)}, f32[1,128,512]{2,1,0:T(8,128)}, u32[]{:S(2)}) copy-start(f32[1,128,512]{2,1,0:T(8,128)} %param.38) | copy-start | bytes 786436
  18.6 26.1 %collective-permute-start.4 = (bf16[128,512]{1,0:T(8,128)(2,1)S(1)}, bf16[128,512]{1,0:T(8,128)(2,1)S(1)}, u32[]{:S(2)}, u32[]{:S(2)}) collective-permute-start(bf16[128,512]{1,0:T(8,128)(2,1)S(1)} %bitcast_convert_fusion.4), channel_id=1, source_target_pairs={{1,0},{2,1},{3,2},{4,3},{5,4},{6,5},{7,6},{8,7},{9,8},{10,9},{11,1... | collective-permute-start | bytes 393224 | tf_op jit(solution)/shard_map/ppermute | solution.py:17
  33.2 22.7 %copy-start.24 = (s32[3]{0:T(128)S(1)}, s32[3]{0:T(128)}, u32[]{:S(2)}) copy-start(s32[3]{0:T(128)} %constant.202.clone.1) | copy-start | bytes 40
  33.3 22.7 %copy-start.29 = (s32[4,3]{1,0:T(4,128)S(1)}, s32[4,3]{1,0:T(4,128)}, u32[]{:S(2)}) copy-start(s32[4,3]{1,0:T(4,128)} %param.31) | copy-start | bytes 148
  33.3 503.0 %all-reduce.6.cloned.1.call-start = ((), (), s32[]{:S(2)}) async-start(), calls=%async_computation | async-start | bytes 2097152 | tf_op jit(solution)/shard_map/psum | solution.py:146
  34.2 11.1 %collective-permute-start.5 = (bf16[128,512]{1,0:T(8,128)(2,1)S(1)}, bf16[128,512]{1,0:T(8,128)(2,1)S(1)}, u32[]{:S(2)}, u32[]{:S(2)}) collective-permute-start(bf16[128,512]{1,0:T(8,128)(2,1)S(1)} %bitcast_convert_fusion.4), channel_id=1, source_target_pairs={{31,0},{0,1},{1,2},{2,3},{3,4},{4,5},{5,6},{6,7},{7,8},{8,9},{9,10... | collective-permute-start | bytes 393224 | tf_op jit(solution)/shard_map/ppermute | solution.py:17
  34.2 11.1 %collective-permute-start.6 = (bf16[128,512]{1,0:T(8,128)(2,1)S(1)}, bf16[128,512]{1,0:T(8,128)(2,1)S(1)}, u32[]{:S(2)}, u32[]{:S(2)}) collective-permute-start(bf16[128,512]{1,0:T(8,128)(2,1)S(1)} %bitcast_convert_fusion.4), channel_id=1, source_target_pairs={{2,0},{3,1},{4,2},{5,3},{6,4},{7,5},{8,6},{9,7},{10,8},{11,9},{12,... | collective-permute-start | bytes 393224 | tf_op jit(solution)/shard_map/ppermute | solution.py:17
  34.6 12.8 %collective-permute-start.7 = (bf16[128,512]{1,0:T(8,128)(2,1)S(1)}, bf16[128,512]{1,0:T(8,128)(2,1)S(1)}, u32[]{:S(2)}, u32[]{:S(2)}) collective-permute-start(bf16[128,512]{1,0:T(8,128)(2,1)S(1)} %bitcast_convert_fusion.4), channel_id=1, source_target_pairs={{30,0},{31,1},{0,2},{1,3},{2,4},{3,5},{4,6},{5,7},{6,8},{7,9},{8,1... | collective-permute-start | bytes 393224 | tf_op jit(solution)/shard_map/ppermute | solution.py:17
  36.3 11.4 %collective-permute-start.8 = (bf16[128,512]{1,0:T(8,128)(2,1)S(1)}, bf16[128,512]{1,0:T(8,128)(2,1)S(1)}, u32[]{:S(2)}, u32[]{:S(2)}) collective-permute-start(bf16[128,512]{1,0:T(8,128)(2,1)S(1)} %bitcast_convert_fusion.3), channel_id=1, source_target_pairs={{1,0},{2,1},{3,2},{4,3},{5,4},{6,5},{7,6},{8,7},{9,8},{10,9},{11,1... | collective-permute-start | bytes 393224 | tf_op jit(solution)/shard_map/ppermute | solution.py:17
  44.7 10.2 %collective-permute-start.9 = (bf16[128,512]{1,0:T(8,128)(2,1)S(1)}, bf16[128,512]{1,0:T(8,128)(2,1)S(1)}, u32[]{:S(2)}, u32[]{:S(2)}) collective-permute-start(bf16[128,512]{1,0:T(8,128)(2,1)S(1)} %bitcast_convert_fusion.3), channel_id=1, source_target_pairs={{31,0},{0,1},{1,2},{2,3},{3,4},{4,5},{5,6},{6,7},{7,8},{8,9},{9,10... | collective-permute-start | bytes 393224 | tf_op jit(solution)/shard_map/ppermute | solution.py:17
  45.3 9.6 collective-permute-start.10
  45.3 10.5 %collective-permute-start.11 = (bf16[128,512]{1,0:T(8,128)(2,1)S(1)}, bf16[128,512]{1,0:T(8,128)(2,1)S(1)}, u32[]{:S(2)}, u32[]{:S(2)}) collective-permute-start(bf16[128,512]{1,0:T(8,128)(2,1)S(1)} %bitcast_convert_fusion.3), channel_id=1, source_target_pairs={{30,0},{31,1},{0,2},{1,3},{2,4},{3,5},{4,6},{5,7},{6,8},{7,9},{8,1... | collective-permute-start | bytes 393224 | tf_op jit(solution)/shard_map/ppermute | solution.py:17
  87.7 39.1 %collective-permute-start.12 = (f32[64,512]{1,0:T(8,128)S(1)}, f32[64,512]{1,0:T(8,128)S(1)}, u32[]{:S(2)}, u32[]{:S(2)}) collective-permute-start(f32[64,512]{1,0:T(8,128)S(1)} %get-tuple-element.389), channel_id=1, source_target_pairs={{31,0},{0,1},{1,2},{2,3},{3,4},{4,5},{5,6},{6,7},{7,8},{8,9},{9,10... | collective-permute-start | bytes 393224 | tf_op jit(solution)/shard_map/ppermute | solution.py:17
  120.7 6.2 collective-permute-start.13
  120.7 9.8 collective-permute-start.14
  122.4 8.6 collective-permute-start.15
  131.0 189.1 %copy-start.22 = (f32[64,512]{1,0:T(8,128)}, f32[64,512]{1,0:T(8,128)S(1)}, u32[]{:S(2)}) copy-start(f32[64,512]{1,0:T(8,128)S(1)} %fusion.191) | copy-start | bytes 393220
  322.6 83.4 %copy-start.15 = (f32[64,512]{1,0:T(8,128)}, f32[64,512]{1,0:T(8,128)S(1)}, u32[]{:S(2)}) copy-start(f32[64,512]{1,0:T(8,128)S(1)} %get-tuple-element.434) | copy-start | bytes 393220
  324.1 3.6 collective-permute-start.16
  325.6 7.3 collective-permute-start.17
  325.7 7.3 collective-permute-start.18
  327.7 7.9 collective-permute-start.19
  366.5 39.5 %copy-start.17 = (f32[64,512]{1,0:T(8,128)S(1)}, f32[64,512]{1,0:T(8,128)}, u32[]{:S(2)}) copy-start(f32[64,512]{1,0:T(8,128)} %get-tuple-element.436) | copy-start | bytes 393220
  368.2 168.1 %copy-start = (f32[512,512]{0,1:T(8,128)S(1)}, f32[512,512]{0,1:T(8,128)}, u32[]{:S(2)}) copy-start(f32[512,512]{0,1:T(8,128)} %get-tuple-element.353) | copy-start | bytes 3145732
  368.2 39.9 %collective-permute-start.20 = (f32[128,512]{1,0:T(8,128)}, f32[128,512]{1,0:T(8,128)}, u32[]{:S(2)}, u32[]{:S(2)}) collective-permute-start(f32[128,512]{1,0:T(8,128)} %get-tuple-element.383), channel_id=1, source_target_pairs={{31,0},{0,1},{1,2},{2,3},{3,4},{4,5},{5,6},{6,7},{7,8},{8,9},{9,10... | collective-permute-start | bytes 786440 | tf_op jit(solution)/shard_map/ppermute | solution.py:17
  400.4 7.7 collective-permute-start.21
  400.4 12.7 %collective-permute-start.22 = (f32[128,512]{1,0:T(8,128)}, f32[128,512]{1,0:T(8,128)}, u32[]{:S(2)}, u32[]{:S(2)}) collective-permute-start(f32[128,512]{1,0:T(8,128)} %get-tuple-element.385), channel_id=1, source_target_pairs={{30,0},{31,1},{0,2},{1,3},{2,4},{3,5},{4,6},{5,7},{6,8},{7,9},{8,1... | collective-permute-start | bytes 786440 | tf_op jit(solution)/shard_map/ppermute | solution.py:17
  402.0 14.1 %collective-permute-start.23 = (f32[128,512]{1,0:T(8,128)}, f32[128,512]{1,0:T(8,128)}, u32[]{:S(2)}, u32[]{:S(2)}) collective-permute-start(f32[128,512]{1,0:T(8,128)} %get-tuple-element.384), channel_id=1, source_target_pairs={{2,0},{3,1},{4,2},{5,3},{6,4},{7,5},{8,6},{9,7},{10,8},{11,9},{12,... | collective-permute-start | bytes 786440 | tf_op jit(solution)/shard_map/ppermute | solution.py:17
  408.1 431.1 %all-reduce.8.cloned.1.call-start = ((), (), s32[]{:S(2)}) async-start(), calls=%async_computation.1 | async-start | bytes 2097152 | tf_op jit(solution)/shard_map/psum | solution.py:167
  690.6 5.0 copy-start.10
  691.5 6.3 collective-permute-start.24
  693.3 8.0 collective-permute-start.25
  693.3 8.0 collective-permute-start.26
  695.2 8.9 collective-permute-start.27
  744.7 47.9 %copy-start.16 = (f32[64,512]{1,0:T(8,128)S(1)}, f32[64,512]{1,0:T(8,128)}, u32[]{:S(2)}) copy-start(f32[64,512]{1,0:T(8,128)} %copy-done.15) | copy-start | bytes 393220
  744.7 47.8 %copy-start.18 = (f32[64,512]{1,0:T(8,128)S(1)}, f32[64,512]{1,0:T(8,128)}, u32[]{:S(2)}) copy-start(f32[64,512]{1,0:T(8,128)} %get-tuple-element.436) | copy-start | bytes 393220
  744.7 48.6 %copy-start.11 = (f32[128,512]{1,0:T(8,128)S(1)}, f32[128,512]{1,0:T(8,128)}, u32[]{:S(2)}) copy-start(f32[128,512]{1,0:T(8,128)} %copy-done.10) | copy-start | bytes 786436
  744.7 48.6 %copy-start.13 = (f32[128,512]{1,0:T(8,128)S(1)}, f32[128,512]{1,0:T(8,128)}, u32[]{:S(2)}) copy-start(f32[128,512]{1,0:T(8,128)} %copy-done.12) | copy-start | bytes 786436
  744.8 94.4 %copy-start.1 = (f32[512,512]{0,1:T(8,128)S(1)}, f32[512,512]{0,1:T(8,128)}, u32[]{:S(2)}) copy-start(f32[512,512]{0,1:T(8,128)} %all-reduce.6.cloned.1.call-done) | copy-start | bytes 3145732
  744.8 49.3 %collective-permute-start.28 = (f32[128,512]{1,0:T(8,128)S(1)}, f32[128,512]{1,0:T(8,128)S(1)}, u32[]{:S(2)}, u32[]{:S(2)}) collective-permute-start(f32[128,512]{1,0:T(8,128)S(1)} %get-tuple-element.379), channel_id=1, source_target_pairs={{31,0},{0,1},{1,2},{2,3},{3,4},{4,5},{5,6},{6,7},{7,8},{8,9},{9,10... | collective-permute-start | bytes 786440 | tf_op jit(solution)/shard_map/ppermute | solution.py:17
  786.9 7.2 collective-permute-start.29
  786.9 12.5 %collective-permute-start.30 = (f32[128,512]{1,0:T(8,128)S(1)}, f32[128,512]{1,0:T(8,128)S(1)}, u32[]{:S(2)}, u32[]{:S(2)}) collective-permute-start(f32[128,512]{1,0:T(8,128)S(1)} %get-tuple-element.381), channel_id=1, source_target_pairs={{30,0},{31,1},{0,2},{1,3},{2,4},{3,5},{4,6},{5,7},{6,8},{7,9},{8,1... | collective-permute-start | bytes 786440 | tf_op jit(solution)/shard_map/ppermute | solution.py:17
  788.6 13.3 %collective-permute-start.31 = (f32[128,512]{1,0:T(8,128)S(1)}, f32[128,512]{1,0:T(8,128)S(1)}, u32[]{:S(2)}, u32[]{:S(2)}) collective-permute-start(f32[128,512]{1,0:T(8,128)S(1)} %get-tuple-element.380), channel_id=1, source_target_pairs={{2,0},{3,1},{4,2},{5,3},{6,4},{7,5},{8,6},{9,7},{10,8},{11,9},{12,... | collective-permute-start | bytes 786440 | tf_op jit(solution)/shard_map/ppermute | solution.py:17
  (17 other events, 35.5 us)
Sparse Core Ops, SparseCore 0:
  33.4 134.1 all-reduce.9
  408.2 128.0 all-reduce.5
  697.8 141.2 all-reduce.7
where the time goes:
time: 1010 us; the launch traced here: 1000 us
  other arithmetic  397 us (39%)
  waiting for transfers between devices  234 us (23%)
  starting transfers between devices  162 us (16%)
  matrix products  95.6 us (9%)
  local copies, waits for them, and re-layouts  43.2 us (4%)
  loops' own time  41 us (4%)
  between operations  29 us (3%)
    another operation x44, other arithmetic, admm_update(): chol_low = jnp.linalg.cholesky(gram_mat + rho_value * identity)  238 us
    ppermute x32, starting transfers between devices, passed_along(): return lax.ppermute(block, axis, route)  162 us
    another operation x7, other arithmetic, chol_solve(): lax.linalg.triangular_solve(chol_low, middle, left_side=True, lower=True,...  119 us
    psum x1, waiting for transfers between devices, per_device(): gram_a = lax.psum(gram_local(factor_a_new), 'dev')  118 us
    ppermute x32, waiting for transfers between devices, passed_along(): return lax.ppermute(block, axis, route)  43 us
    psum x1, waiting for transfers between devices, per_device(): lax.psum((gram_local(factor_b), gram_local(factor_c)), 'dev')  36.6 us
    psum x1, waiting for transfers between devices, per_device(): gram_bn = lax.psum(gram_local(factor_b_new), 'dev')  36.4 us
    another operation x40, local copies, waits for them, and re-layouts, chol_solve(): lax.linalg.triangular_solve(chol_low, middle, left_side=True, lower=True,...  24.3 us
  transfers between devices with their start and end apart: 35, of which 17 were waited for; matrix products, arithmetic and copies ran while one was open for 6% of the time, Pallas kernels for 0%

commit v1 on v0

--- a/solution.py
+++ b/solution.py
@@ -143,7 +143,11 @@
     factor_a_new, dual_a_new = admm_update(
         mttkrp_a, factor_a[0], dual_a[0], gram_b * gram_c, penalty[0]
     )
-    gram_a = lax.psum(gram_local(factor_a_new), "dev")
+
+    def expand_edges(work_x):
+        return lax.all_gather(work_x, axis_name="dev").sum(axis=0)
+
+    gram_a = expand_edges(gram_local(factor_a_new))
     second_window = expand((factor_a_new.astype(jnp.bfloat16),))
     win_a = jnp.stack([member[0] for member in second_window])
 

time: 1010 us -> 1040 us (1.030)
  other arithmetic: 397 us -> 425 us
  waiting for transfers between devices: 234 us -> 212 us
  local copies, waits for them, and re-layouts: 43.2 us -> 60.2 us
    psum x1 -> x0, waiting for transfers between devices: 118 us -> none  [per_device(): gram_a = lax.psum(gram_local(factor_a_new), 'dev')]
    all_gather x0 -> x1, waiting for transfers between devices: none -> 110 us  [expand_edges(): return lax.all_gather(work_x, axis_name='dev').sum(axis=0)]
    psum x1, waiting for transfers between devices: 36.4 us -> 21.3 us  [per_device(): gram_bn = lax.psum(gram_local(factor_b_new), 'dev')]
    reduce_sum x0 -> x1, other arithmetic: none -> 12.3 us  [expand_edges(): return lax.all_gather(work_x, axis_name='dev').sum(axis=0)]
  transfers between devices with their start and end apart: 35 -> 35, of which waited for: 17 -> 17; matrix products, arithmetic and copies ran while one was open for 6% -> 9% of each run, Pallas kernels for 0% -> 0%
where the time goes in v1:
time: 1040 us; the launch traced here: 1030 us
  other arithmetic  425 us (41%)
  waiting for transfers between devices  212 us (20%)
  starting transfers between devices  169 us (16%)
  matrix products  96.5 us (9%)
  local copies, waits for them, and re-layouts  60.2 us (6%)
  loops' own time  40.1 us (4%)
  between operations  28.9 us (3%)
    another operation x44, other arithmetic, admm_update(): chol_low = jnp.linalg.cholesky(gram_mat + rho_value * identity)  244 us
    ppermute x32, starting transfers between devices, passed_along(): return lax.ppermute(block, axis, route)  169 us
    another operation x7, other arithmetic, chol_solve(): lax.linalg.triangular_solve(chol_low, middle, left_side=True, lower=True,...  121 us
    all_gather x1, waiting for transfers between devices, expand_edges(): return lax.all_gather(work_x, axis_name='dev').sum(axis=0)  110 us
    ppermute x32, waiting for transfers between devices, passed_along(): return lax.ppermute(block, axis, route)  49.3 us
    psum x1, waiting for transfers between devices, per_device(): lax.psum((gram_local(factor_b), gram_local(factor_c)), 'dev')  31.4 us
    another operation x40, local copies, waits for them, and re-layouts, chol_solve(): lax.linalg.triangular_solve(chol_low, middle, left_side=True, lower=True,...  31.1 us
    psum x1, waiting for transfers between devices, per_device(): gram_bn = lax.psum(gram_local(factor_b_new), 'dev')  21.3 us
  transfers between devices with their start and end apart: 35, of which 17 were waited for; matrix products, arithmetic and copies ran while one was open for 9% of the time, Pallas kernels for 0%

profile of v1, /device:TPU:0, one launch (start us, length us, event | category | flops | bytes accessed | tf_op | source)
XLA Modules:
  0.0 1031.4 jit_solution(15153921139527722520)
XLA Ops:
  9.2 6.4 collective-permute-start
  18.6 8.4 collective-permute-start.4
  36.3 8.3 collective-permute-start.8
  47.7 7.3 collective-permute-done.9
  56.0 31.6 %while.45 = (s32[]{:T(128)}, f32[5,64,512]{2,1,0:T(8,128)S(1)}, s32[]{:T(128)}, s32[5,3]{0,1:T(4,128)S(1)}, s32[4,3]{1,0:T(4,128)}, /*index=5*/bf16[4,64,128,128...) while((s32[]{:T(128)}, f32[5,64,512]{2,1,0:T(8,128)S(1)}, ...), condition=%wide.region_6.7_spmd, body=%wide.region_0.6_spmd.sunk | while | flops 1082228736 | bytes 3408323 | solution.py:141
  88.5 15.9 %collective-permute-start.15 = (f32[64,512]{1,0:T(8,128)S(1)}, f32[64,512]{1,0:T(8,128)S(1)}, u32[]{:S(2)}, u32[]{:S(2)}) collective-permute-start(f32[64,512]{1,0:T(8,128)S(1)} %get-tuple-element.414), channel_id=1, source_target_pairs={{2,0},{3,1},{4,2},{5,3},{6,4},{7,5},{8,6},{9,7},{10,8},{11,9},{12,... | collective-permute-start | bytes 393224 | tf_op jit(solution)/shard_map/ppermute | solution.py:17
  104.5 23.0 %collective-permute-start.13 = (f32[64,512]{1,0:T(8,128)S(1)}, f32[64,512]{1,0:T(8,128)S(1)}, u32[]{:S(2)}, u32[]{:S(2)}) collective-permute-start(f32[64,512]{1,0:T(8,128)S(1)} %get-tuple-element.416), channel_id=1, source_target_pairs={{1,0},{2,1},{3,2},{4,3},{5,4},{6,5},{7,6},{8,7},{9,8},{10,9},{11,1... | collective-permute-start | bytes 393224 | tf_op jit(solution)/shard_map/ppermute | solution.py:17
  130.2 6.1 collective-permute-done.12
  137.0 31.4 %all-reduce.7.cloned.1.call-done = (f32[512,512]{0,1:T(8,128)}, f32[512,512]{0,1:T(8,128)}) async-done(((f32[512,512]{0,1:T(8,128)}, f32[512,512]{0,1:T(8,128)}), (f32[512,512]{0,1:T(8,128)}, f32[512,512]{0,1:T(8,128)})) %all-reduce.7.cloned.1.call-update) | async-done | bytes 2097168 | tf_op jit(solution)/shard_map/psum | solution.py:112
  175.9 11.7 %cholesky.374 = f32[128,128]{1,0:T(8,128)S(1)} custom-call(f32[128,128]{1,0:T(8,128)S(1)} %cholesky.586), custom_call_target="Cholesky" | custom-call | tf_op jit(solution)/shard_map/jit(cholesky)/cholesky | solution.py:79
  187.8 9.8 custom-call.36
  200.1 11.7 %cholesky.393 = f32[128,128]{1,0:T(8,128)S(1)} custom-call(f32[128,128]{1,0:T(8,128)S(1)} %cholesky.590), custom_call_target="Cholesky" | custom-call | tf_op jit(solution)/shard_map/jit(cholesky)/cholesky | solution.py:79
  211.9 9.9 custom-call.37
  223.4 11.7 %cholesky.414 = f32[128,128]{1,0:T(8,128)S(1)} custom-call(f32[128,128]{1,0:T(8,128)S(1)} %cholesky.595), custom_call_target="Cholesky" | custom-call | tf_op jit(solution)/shard_map/jit(cholesky)/cholesky | solution.py:79
  235.2 9.8 custom-call.38
  246.4 11.7 %cholesky.431 = f32[128,128]{1,0:T(8,128)S(1)} custom-call(f32[128,128]{1,0:T(8,128)S(1)} %convolution_subtract_fusion.26), custom_call_target="Cholesky" | custom-call | tf_op jit(solution)/shard_map/jit(cholesky)/cholesky | solution.py:79
  262.8 8.0 while.48
  270.9 39.7 %custom-call.40 = f32[4,128,128]{1,2,0:T(8,128)S(1)} custom-call(f32[4,128,128]{2,1,0:T(8,128)S(1)} %get-tuple-element.218), custom_call_target="InvertDiagBlocksLowerTriangular" | custom-call | tf_op jit(solution)/shard_map/triangular_solve/custom-call.8 | solution.py:22
  338.4 33.6 %while.46 = (s32[]{:T(128)}, f32[5,128,512]{2,1,0:T(8,128)S(1)}, s32[]{:T(128)}, s32[5,3]{0,1:T(4,128)S(1)}, s32[4,3]{1,0:T(4,128)}, /*index=5*/bf16[4,64,128,12...) while((s32[]{:T(128)}, f32[5,128,512]{2,1,0:T(8,128)S(1)}, ...), condition=%wide.region_24.28_spmd, body=%wide.region_18.27_spmd.sunk | while | flops 1082228736 | bytes 3604931 | solution.py:166
  372.9 16.6 %collective-permute-start.23 = (f32[128,512]{1,0:T(8,128)}, f32[128,512]{1,0:T(8,128)S(1)}, u32[]{:S(2)}, u32[]{:S(2)}) collective-permute-start(f32[128,512]{1,0:T(8,128)} %get-tuple-element.408), channel_id=1, source_target_pairs={{2,0},{3,1},{4,2},{5,3},{6,4},{7,5},{8,6},{9,7},{10,8},{11,9},{12,... | collective-permute-start | bytes 786440 | tf_op jit(solution)/shard_map/ppermute | solution.py:17
  389.5 22.8 %collective-permute-start.21 = (f32[128,512]{1,0:T(8,128)}, f32[128,512]{1,0:T(8,128)S(1)}, u32[]{:S(2)}, u32[]{:S(2)}) collective-permute-start(f32[128,512]{1,0:T(8,128)} %get-tuple-element.410), channel_id=1, source_target_pairs={{1,0},{2,1},{3,2},{4,3},{5,4},{6,5},{7,6},{8,7},{9,8},{10,9},{11,1... | collective-permute-start | bytes 786440 | tf_op jit(solution)/shard_map/ppermute | solution.py:17
  412.4 10.8 %collective-permute-done.21 = f32[128,512]{1,0:T(8,128)S(1)} collective-permute-done((f32[128,512]{1,0:T(8,128)}, f32[128,512]{1,0:T(8,128)S(1)}, u32[]{:S(2)}, u32[]{:S(2)}) %collective-permute-start.21) | collective-permute-done | bytes 262176 | tf_op jit(solution)/shard_map/ppermute | solution.py:17
  428.4 110.0 %all-gather.3.cloned.1.call-done = f32[16384,512]{1,0:T(8,128)} async-done(((f32[512,512]{1,0:T(8,128)}), f32[16384,512]{1,0:T(8,128)}) %all-gather.3.cloned.1.call-update) | async-done | bytes 33554448 | tf_op jit(solution)/shard_map/all_gather | solution.py:148
  538.4 12.3 %reduce_sum.140 = f32[512,512]{1,0:T(8,128)S(1)} reduce(f32[32,512,512]{2,1,0:T(8,128)} %bitcast.569, f32[]{:T(128)} %constant.235.clone.1), dimensions={0}, to_apply=%region_25.29 | reduce | flops 8126464 | bytes 34603012 | tf_op jit(solution)/shard_map/reduce_sum | solution.py:148
  560.4 11.7 %cholesky.446 = f32[128,128]{1,0:T(8,128)S(1)} custom-call(f32[128,128]{1,0:T(8,128)S(1)} %cholesky.599), custom_call_target="Cholesky" | custom-call | tf_op jit(solution)/shard_map/jit(cholesky)/cholesky | solution.py:79
  572.3 9.8 custom-call.41
  585.3 11.7 %cholesky.465 = f32[128,128]{1,0:T(8,128)S(1)} custom-call(f32[128,128]{1,0:T(8,128)S(1)} %cholesky.603), custom_call_target="Cholesky" | custom-call | tf_op jit(solution)/shard_map/jit(cholesky)/cholesky | solution.py:79
  597.6 10.2 custom-call.42
  610.9 13.2 %cholesky.486 = f32[128,128]{1,0:T(8,128)} custom-call(f32[128,128]{1,0:T(8,128)} %cholesky.608), custom_call_target="Cholesky" | custom-call | tf_op jit(solution)/shard_map/jit(cholesky)/cholesky | solution.py:79
  626.1 11.3 %custom-call.43 = f32[1,128,128]{1,2,0:T(8,128)} custom-call(f32[1,128,128]{2,1,0:T(8,128)} %get-tuple-element.434), custom_call_target="InvertDiagBlocksLowerTriangular" | custom-call | tf_op jit(solution)/shard_map/jit(cholesky)/cholesky | solution.py:79
  639.7 11.9 %cholesky.503 = f32[128,128]{1,0:T(8,128)S(1)} custom-call(f32[128,128]{1,0:T(8,128)S(1)} %convolution_subtract_fusion.25), custom_call_target="Cholesky" | custom-call | tf_op jit(solution)/shard_map/jit(cholesky)/cholesky | solution.py:79
  659.9 14.0 %while.49 = (s32[]{:T(128)}, f32[512,512]{1,0:T(8,128)}, s32[4,2]{0,1:T(2,128)S(1)}, f32[4,128,128]{2,1,0:T(8,128)}, s32[]{:T(128)}) while((s32[]{:T(128)}, f32[512,512]{1,0:T(8,128)}, s32[4,2]{0,1:T(2,128)S(1)}, f32[4,128,128]{2,1,0:T(8,128)}, s32[]{:T(128)}) %tuple.226), condition=%wide.while_cond.4.clone, body=%wide.while_body.4.clone.sunk | while | flops 2 | bytes 132205 | solution.py:22
  673.9 40.8 %custom-call.45 = f32[4,128,128]{1,2,0:T(8,128)} custom-call(f32[4,128,128]{2,1,0:T(8,128)} %get-tuple-element.220), custom_call_target="InvertDiagBlocksLowerTriangular" | custom-call | tf_op jit(solution)/shard_map/triangular_solve/custom-call.8 | solution.py:22
  744.0 45.0 %while.47 = (s32[]{:T(128)}, f32[5,128,512]{2,1,0:T(8,128)S(1)}, s32[]{:T(128)}, s32[5,3]{0,1:T(4,128)S(1)}, s32[4,3]{1,0:T(4,128)}, /*index=5*/bf16[4,64,128,12...) while((s32[]{:T(128)}, f32[5,128,512]{2,1,0:T(8,128)S(1)}, ...), condition=%wide.region_33.37_spmd, body=%wide.region_27.36_spmd.sunk | while | flops 1090650112 | bytes 9109983 | solution.py:190
  758.0 6.8 multiply_reduce_fusion.8
  780.2 6.8 multiply_reduce_fusion.8
  789.2 24.7 %collective-permute-start.31 = (f32[128,512]{1,0:T(8,128)S(1)}, f32[128,512]{1,0:T(8,128)S(1)}, u32[]{:S(2)}, u32[]{:S(2)}) collective-permute-start(f32[128,512]{1,0:T(8,128)S(1)} %get-tuple-element.404), channel_id=1, source_target_pairs={{2,0},{3,1},{4,2},{5,3},{6,4},{7,5},{8,6},{9,7},{10,8},{11,9},{12,... | collective-permute-start | bytes 786440 | tf_op jit(solution)/shard_map/ppermute | solution.py:17
  813.9 27.6 %collective-permute-start.29 = (f32[128,512]{1,0:T(8,128)S(1)}, f32[128,512]{1,0:T(8,128)S(1)}, u32[]{:S(2)}, u32[]{:S(2)}) collective-permute-start(f32[128,512]{1,0:T(8,128)S(1)} %get-tuple-element.406), channel_id=1, source_target_pairs={{1,0},{2,1},{3,2},{4,3},{5,4},{6,5},{7,6},{8,7},{9,8},{10,9},{11,1... | collective-permute-start | bytes 786440 | tf_op jit(solution)/shard_map/ppermute | solution.py:17
  851.7 21.3 %all-reduce.5.cloned.1.call-done = f32[512,512]{0,1:T(8,128)} async-done(((f32[512,512]{0,1:T(8,128)}), f32[512,512]{0,1:T(8,128)}) %all-reduce.5.cloned.1.call-update) | async-done | bytes 1048592 | tf_op jit(solution)/shard_map/psum | solution.py:171
  879.2 11.7 %cholesky.518 = f32[128,128]{1,0:T(8,128)S(1)} custom-call(f32[128,128]{1,0:T(8,128)S(1)} %cholesky.612), custom_call_target="Cholesky" | custom-call | tf_op jit(solution)/shard_map/jit(cholesky)/cholesky | solution.py:79
  891.1 9.8 custom-call.46
  901.5 11.7 %cholesky.537 = f32[128,128]{1,0:T(8,128)S(1)} custom-call(f32[128,128]{1,0:T(8,128)S(1)} %cholesky.616), custom_call_target="Cholesky" | custom-call | tf_op jit(solution)/shard_map/jit(cholesky)/cholesky | solution.py:79
  913.3 10.0 custom-call.47
  923.9 11.7 %cholesky.558 = f32[128,128]{1,0:T(8,128)S(1)} custom-call(f32[128,128]{1,0:T(8,128)S(1)} %cholesky.621), custom_call_target="Cholesky" | custom-call | tf_op jit(solution)/shard_map/jit(cholesky)/cholesky | solution.py:79
  935.7 9.8 custom-call.48
  946.1 11.9 %cholesky.575 = f32[128,128]{1,0:T(8,128)S(1)} custom-call(f32[128,128]{1,0:T(8,128)S(1)} %convolution_subtract_fusion.24), custom_call_target="Cholesky" | custom-call | tf_op jit(solution)/shard_map/jit(cholesky)/cholesky | solution.py:79
  963.4 8.5 while.50
  971.8 39.3 %custom-call.50 = f32[4,128,128]{1,2,0:T(8,128)S(1)} custom-call(f32[4,128,128]{2,1,0:T(8,128)S(1)} %get-tuple-element.222), custom_call_target="InvertDiagBlocksLowerTriangular" | custom-call | tf_op jit(solution)/shard_map/triangular_solve/custom-call.8 | solution.py:22
  (367 shorter events, 243.4 us)
Async XLA Ops:
  7.2 161.2 %all-reduce.7.cloned.1.call-start = ((), (), s32[]{:S(2)}) async-start(), calls=%async_computation.2 | async-start | bytes 4194304 | tf_op jit(solution)/shard_map/psum | solution.py:112
  9.2 25.0 %collective-permute-start = (s32[3]{0:T(128)S(1)}, s32[3]{0:T(128)S(1)}, u32[]{:S(2)}, u32[]{:S(2)}) collective-permute-start(s32[3]{0:T(128)S(1)} %pad_add_fusion), channel_id=1, source_target_pairs={{1,0},{2,1},{3,2},{4,3},{5,4},{6,5},{7,6},{8,7},{9,8},{10,9},{11,1... | collective-permute-start | bytes 44 | tf_op jit(solution)/shard_map/ppermute | solution.py:17
  15.6 18.6 %collective-permute-start.1 = (s32[3]{0:T(128)S(1)}, s32[3]{0:T(128)S(1)}, u32[]{:S(2)}, u32[]{:S(2)}) collective-permute-start(s32[3]{0:T(128)S(1)} %pad_add_fusion), channel_id=1, source_target_pairs={{31,0},{0,1},{1,2},{2,3},{3,4},{4,5},{5,6},{6,7},{7,8},{8,9},{9,10... | collective-permute-start | bytes 44 | tf_op jit(solution)/shard_map/ppermute | solution.py:17
  15.6 19.0 %collective-permute-start.2 = (s32[3]{0:T(128)S(1)}, s32[3]{0:T(128)S(1)}, u32[]{:S(2)}, u32[]{:S(2)}) collective-permute-start(s32[3]{0:T(128)S(1)} %pad_add_fusion), channel_id=1, source_target_pairs={{2,0},{3,1},{4,2},{5,3},{6,4},{7,5},{8,6},{9,7},{10,8},{11,9},{12,... | collective-permute-start | bytes 44 | tf_op jit(solution)/shard_map/ppermute | solution.py:17
  16.7 19.6 %collective-permute-start.3 = (s32[3]{0:T(128)S(1)}, s32[3]{0:T(128)S(1)}, u32[]{:S(2)}, u32[]{:S(2)}) collective-permute-start(s32[3]{0:T(128)S(1)} %pad_add_fusion), channel_id=1, source_target_pairs={{30,0},{31,1},{0,2},{1,3},{2,4},{3,5},{4,6},{5,7},{6,8},{7,9},{8,1... | collective-permute-start | bytes 44 | tf_op jit(solution)/shard_map/ppermute | solution.py:17
  18.6 14.8 %copy-start.5 = (f32[1,128,512]{2,1,0:T(8,128)S(1)}, f32[1,128,512]{2,1,0:T(8,128)}, u32[]{:S(2)}) copy-start(f32[1,128,512]{2,1,0:T(8,128)} %param.38) | copy-start | bytes 786436
  18.6 26.1 %collective-permute-start.4 = (bf16[128,512]{1,0:T(8,128)(2,1)S(1)}, bf16[128,512]{1,0:T(8,128)(2,1)S(1)}, u32[]{:S(2)}, u32[]{:S(2)}) collective-permute-start(bf16[128,512]{1,0:T(8,128)(2,1)S(1)} %bitcast_convert_fusion.4), channel_id=1, source_target_pairs={{1,0},{2,1},{3,2},{4,3},{5,4},{6,5},{7,6},{8,7},{9,8},{10,9},{11,1... | collective-permute-start | bytes 393224 | tf_op jit(solution)/shard_map/ppermute | solution.py:17
  30.1 3.4 copy-start.24
  33.3 22.7 %copy-start.22 = (s32[3]{0:T(128)S(1)}, s32[3]{0:T(128)}, u32[]{:S(2)}) copy-start(s32[3]{0:T(128)} %constant.203.clone.1) | copy-start | bytes 40
  33.3 505.1 %all-gather.3.cloned.1.call-start = ((), (), s32[]{:S(2)}) async-start(), calls=%async_computation.1 | async-start | bytes 34603008 | tf_op jit(solution)/shard_map/all_gather | solution.py:148
  34.2 11.1 %collective-permute-start.5 = (bf16[128,512]{1,0:T(8,128)(2,1)S(1)}, bf16[128,512]{1,0:T(8,128)(2,1)S(1)}, u32[]{:S(2)}, u32[]{:S(2)}) collective-permute-start(bf16[128,512]{1,0:T(8,128)(2,1)S(1)} %bitcast_convert_fusion.4), channel_id=1, source_target_pairs={{31,0},{0,1},{1,2},{2,3},{3,4},{4,5},{5,6},{6,7},{7,8},{8,9},{9,10... | collective-permute-start | bytes 393224 | tf_op jit(solution)/shard_map/ppermute | solution.py:17
  34.3 11.2 %collective-permute-start.6 = (bf16[128,512]{1,0:T(8,128)(2,1)S(1)}, bf16[128,512]{1,0:T(8,128)(2,1)S(1)}, u32[]{:S(2)}, u32[]{:S(2)}) collective-permute-start(bf16[128,512]{1,0:T(8,128)(2,1)S(1)} %bitcast_convert_fusion.4), channel_id=1, source_target_pairs={{2,0},{3,1},{4,2},{5,3},{6,4},{7,5},{8,6},{9,7},{10,8},{11,9},{12,... | collective-permute-start | bytes 393224 | tf_op jit(solution)/shard_map/ppermute | solution.py:17
  34.7 12.8 %collective-permute-start.7 = (bf16[128,512]{1,0:T(8,128)(2,1)S(1)}, bf16[128,512]{1,0:T(8,128)(2,1)S(1)}, u32[]{:S(2)}, u32[]{:S(2)}) collective-permute-start(bf16[128,512]{1,0:T(8,128)(2,1)S(1)} %bitcast_convert_fusion.4), channel_id=1, source_target_pairs={{30,0},{31,1},{0,2},{1,3},{2,4},{3,5},{4,6},{5,7},{6,8},{7,9},{8,1... | collective-permute-start | bytes 393224 | tf_op jit(solution)/shard_map/ppermute | solution.py:17
  36.3 11.4 %collective-permute-start.8 = (bf16[128,512]{1,0:T(8,128)(2,1)S(1)}, bf16[128,512]{1,0:T(8,128)(2,1)S(1)}, u32[]{:S(2)}, u32[]{:S(2)}) collective-permute-start(bf16[128,512]{1,0:T(8,128)(2,1)S(1)} %bitcast_convert_fusion.3), channel_id=1, source_target_pairs={{1,0},{2,1},{3,2},{4,3},{5,4},{6,5},{7,6},{8,7},{9,8},{10,9},{11,1... | collective-permute-start | bytes 393224 | tf_op jit(solution)/shard_map/ppermute | solution.py:17
  44.8 10.2 collective-permute-start.9
  45.4 9.6 collective-permute-start.10
  45.4 10.5 %collective-permute-start.11 = (bf16[128,512]{1,0:T(8,128)(2,1)S(1)}, bf16[128,512]{1,0:T(8,128)(2,1)S(1)}, u32[]{:S(2)}, u32[]{:S(2)}) collective-permute-start(bf16[128,512]{1,0:T(8,128)(2,1)S(1)} %bitcast_convert_fusion.3), channel_id=1, source_target_pairs={{30,0},{31,1},{0,2},{1,3},{2,4},{3,5},{4,6},{5,7},{6,8},{7,9},{8,1... | collective-permute-start | bytes 393224 | tf_op jit(solution)/shard_map/ppermute | solution.py:17
  88.5 39.5 %collective-permute-start.15 = (f32[64,512]{1,0:T(8,128)S(1)}, f32[64,512]{1,0:T(8,128)S(1)}, u32[]{:S(2)}, u32[]{:S(2)}) collective-permute-start(f32[64,512]{1,0:T(8,128)S(1)} %get-tuple-element.414), channel_id=1, source_target_pairs={{2,0},{3,1},{4,2},{5,3},{6,4},{7,5},{8,6},{9,7},{10,8},{11,9},{12,... | collective-permute-start | bytes 393224 | tf_op jit(solution)/shard_map/ppermute | solution.py:17
  104.4 23.6 %collective-permute-start.14 = (f32[64,512]{1,0:T(8,128)S(1)}, f32[64,512]{1,0:T(8,128)S(1)}, u32[]{:S(2)}, u32[]{:S(2)}) collective-permute-start(f32[64,512]{1,0:T(8,128)S(1)} %get-tuple-element.415), channel_id=1, source_target_pairs={{30,0},{31,1},{0,2},{1,3},{2,4},{3,5},{4,6},{5,7},{6,8},{7,9},{8,1... | collective-permute-start | bytes 393224 | tf_op jit(solution)/shard_map/ppermute | solution.py:17
  104.5 25.8 %collective-permute-start.13 = (f32[64,512]{1,0:T(8,128)S(1)}, f32[64,512]{1,0:T(8,128)S(1)}, u32[]{:S(2)}, u32[]{:S(2)}) collective-permute-start(f32[64,512]{1,0:T(8,128)S(1)} %get-tuple-element.416), channel_id=1, source_target_pairs={{1,0},{2,1},{3,2},{4,3},{5,4},{6,5},{7,6},{8,7},{9,8},{10,9},{11,1... | collective-permute-start | bytes 393224 | tf_op jit(solution)/shard_map/ppermute | solution.py:17
  127.4 8.9 collective-permute-start.12
  322.5 3.5 copy-start.15
  323.9 14.5 %copy-start.17 = (f32[64,512]{1,0:T(8,128)}, f32[64,512]{1,0:T(8,128)S(1)}, u32[]{:S(2)}) copy-start(f32[64,512]{1,0:T(8,128)S(1)} %get-tuple-element.460) | copy-start | bytes 393220
  326.0 547.0 %all-reduce.5.cloned.1.call-start = ((), (), s32[]{:S(2)}) async-start(), calls=%async_computation | async-start | bytes 2097152 | tf_op jit(solution)/shard_map/psum | solution.py:171
  326.0 3.6 collective-permute-start.16
  327.6 7.3 collective-permute-start.17
  327.6 7.9 collective-permute-start.18
  329.6 8.0 collective-permute-start.19
  372.9 39.4 %collective-permute-start.23 = (f32[128,512]{1,0:T(8,128)}, f32[128,512]{1,0:T(8,128)S(1)}, u32[]{:S(2)}, u32[]{:S(2)}) collective-permute-start(f32[128,512]{1,0:T(8,128)} %get-tuple-element.408), channel_id=1, source_target_pairs={{2,0},{3,1},{4,2},{5,3},{6,4},{7,5},{8,6},{9,7},{10,8},{11,9},{12,... | collective-permute-start | bytes 786440 | tf_op jit(solution)/shard_map/ppermute | solution.py:17
  389.5 22.9 %collective-permute-start.22 = (f32[128,512]{1,0:T(8,128)}, f32[128,512]{1,0:T(8,128)S(1)}, u32[]{:S(2)}, u32[]{:S(2)}) collective-permute-start(f32[128,512]{1,0:T(8,128)} %get-tuple-element.409), channel_id=1, source_target_pairs={{30,0},{31,1},{0,2},{1,3},{2,4},{3,5},{4,6},{5,7},{6,8},{7,9},{8,1... | collective-permute-start | bytes 786440 | tf_op jit(solution)/shard_map/ppermute | solution.py:17
  389.5 33.6 %collective-permute-start.21 = (f32[128,512]{1,0:T(8,128)}, f32[128,512]{1,0:T(8,128)S(1)}, u32[]{:S(2)}, u32[]{:S(2)}) collective-permute-start(f32[128,512]{1,0:T(8,128)} %get-tuple-element.410), channel_id=1, source_target_pairs={{1,0},{2,1},{3,2},{4,3},{5,4},{6,5},{7,6},{8,7},{9,8},{10,9},{11,1... | collective-permute-start | bytes 786440 | tf_op jit(solution)/shard_map/ppermute | solution.py:17
  412.4 14.3 %collective-permute-start.20 = (f32[128,512]{1,0:T(8,128)}, f32[128,512]{1,0:T(8,128)}, u32[]{:S(2)}, u32[]{:S(2)}) collective-permute-start(f32[128,512]{1,0:T(8,128)} %get-tuple-element.407), channel_id=1, source_target_pairs={{31,0},{0,1},{1,2},{2,3},{3,4},{4,5},{5,6},{6,7},{7,8},{8,9},{9,10... | collective-permute-start | bytes 786440 | tf_op jit(solution)/shard_map/ppermute | solution.py:17
  673.9 44.9 %copy-start.1 = (f32[512,512]{1,0:T(8,128)S(1)}, f32[512,512]{1,0:T(8,128)}, u32[]{:S(2)}) copy-start(f32[512,512]{1,0:T(8,128)} %get-tuple-element.929) | copy-start | bytes 3145732
  714.8 5.1 copy-start.12
  729.2 6.0 copy-start.8
  730.7 4.6 copy-start.10
  730.7 6.6 collective-permute-start.24
  732.8 8.0 collective-permute-start.25
  732.8 8.6 collective-permute-start.26
  734.3 8.9 collective-permute-start.27
  789.1 52.4 %copy-start.16 = (f32[64,512]{1,0:T(8,128)S(1)}, f32[64,512]{1,0:T(8,128)}, u32[]{:S(2)}) copy-start(f32[64,512]{1,0:T(8,128)} %copy-done.15) | copy-start | bytes 393220
  789.1 52.4 %copy-start.18 = (f32[64,512]{1,0:T(8,128)S(1)}, f32[64,512]{1,0:T(8,128)}, u32[]{:S(2)}) copy-start(f32[64,512]{1,0:T(8,128)} %copy-done.17) | copy-start | bytes 393220
  789.1 53.1 %copy-start.9 = (f32[128,512]{1,0:T(8,128)S(1)}, f32[128,512]{1,0:T(8,128)}, u32[]{:S(2)}) copy-start(f32[128,512]{1,0:T(8,128)} %copy-done.8) | copy-start | bytes 786436
  789.1 53.1 %copy-start.11 = (f32[128,512]{1,0:T(8,128)S(1)}, f32[128,512]{1,0:T(8,128)}, u32[]{:S(2)}) copy-start(f32[128,512]{1,0:T(8,128)} %copy-done.10) | copy-start | bytes 786436
  789.2 53.9 %collective-permute-start.31 = (f32[128,512]{1,0:T(8,128)S(1)}, f32[128,512]{1,0:T(8,128)S(1)}, u32[]{:S(2)}, u32[]{:S(2)}) collective-permute-start(f32[128,512]{1,0:T(8,128)S(1)} %get-tuple-element.404), channel_id=1, source_target_pairs={{2,0},{3,1},{4,2},{5,3},{6,4},{7,5},{8,6},{9,7},{10,8},{11,9},{12,... | collective-permute-start | bytes 786440 | tf_op jit(solution)/shard_map/ppermute | solution.py:17
  813.9 29.2 %collective-permute-start.30 = (f32[128,512]{1,0:T(8,128)S(1)}, f32[128,512]{1,0:T(8,128)S(1)}, u32[]{:S(2)}, u32[]{:S(2)}) collective-permute-start(f32[128,512]{1,0:T(8,128)S(1)} %get-tuple-element.405), channel_id=1, source_target_pairs={{30,0},{31,1},{0,2},{1,3},{2,4},{3,5},{4,6},{5,7},{6,8},{7,9},{8,1... | collective-permute-start | bytes 786440 | tf_op jit(solution)/shard_map/ppermute | solution.py:17
  813.9 31.5 %collective-permute-start.29 = (f32[128,512]{1,0:T(8,128)S(1)}, f32[128,512]{1,0:T(8,128)S(1)}, u32[]{:S(2)}, u32[]{:S(2)}) collective-permute-start(f32[128,512]{1,0:T(8,128)S(1)} %get-tuple-element.406), channel_id=1, source_target_pairs={{1,0},{2,1},{3,2},{4,3},{5,4},{6,5},{7,6},{8,7},{9,8},{10,9},{11,1... | collective-permute-start | bytes 786440 | tf_op jit(solution)/shard_map/ppermute | solution.py:17
  841.4 9.4 collective-permute-start.28
  (15 other events, 28.9 us)
Sparse Core Ops, SparseCore 0:
  33.4 134.8 all-reduce.6
  326.1 212.3 all-gather.2
  737.5 135.4 all-reduce.4
